TPU v7x, 32 devices: a whole 2x2x4 slice. The times are simulated.
32 devices in a mesh: replica: 8 (over y, x, core), fsdp: 4 (over z).
Axes of the slice: x: 2, y: 2, z: 4, core: 2. Of those that a mesh axis runs over, the one named last changes fastest.
Arguments:
- tokens: bfloat16 [6144, 4096], P(('replica', 'fsdp')), may hold values from -6 to 6
- grads_out: bfloat16 [6144, 1024], P(('replica', 'fsdp')), may hold values from -6 to 6
- weights: bfloat16 [8, 4096, 1024], P('replica', 'fsdp'), may hold values from -0.29882812 to 0.29882812
- moments: float32 [8, 4096, 1024], P('replica', 'fsdp'), may hold values from -6 to 6
- step: int32 [1], replicated, may hold values from 0 to 999
Outputs:
- mixed_weights: bfloat16 [8, 4096, 1024], P('replica', 'fsdp')
- new_moments: float32 [8, 4096, 1024], P('replica', 'fsdp')
All inputs are finite; a program needn't handle non-finite values.
Results may differ from a plain program's by a relative error of at most 0.001.
Values may be sent and summed in bfloat16 or wider, within the bound.
No kernel may reach another device: no remote copies, remote signals or barrier semaphores. Data moves between devices by JAX's collectives and lax.ppermute only.
A program may use at most 64 MiB of HBM per device.

v0:
```python
from functools import partial

import jax
import jax.numpy as jnp
from jax import lax
from jax.sharding import PartitionSpec as P


def from_behind(block, axis, distance):
    devices = range(lax.axis_size(axis))
    route = [((i - distance) % len(devices), i) for i in devices]
    return lax.ppermute(block, axis, route)


def jump_by(state, reach):
    return from_behind(state, "replica", reach)


def body(tokens, grads_out, weights, moments, step):
    features = lax.all_to_all(tokens, "fsdp", split_axis=1, concat_axis=0, tiled=True)
    gradient = lax.dot_general(
        features,
        lax.all_gather(grads_out, "fsdp", axis=0, tiled=True),
        (((0,), (0,)), ((), ())),
        preferred_element_type=jnp.float32,
    )
    total_tokens = tokens.shape[0] * lax.axis_size("fsdp")
    gradient = gradient * jnp.float32(total_tokens ** (-0.5))
    new_moments = 0.9 * moments[0] + gradient
    updated = weights[0].astype(jnp.float32) - 0.05 * new_moments
    levels = lax.axis_size("replica").bit_length() - 1
    level = step[0] % levels
    branches = [partial(jump_by, reach=1 << power) for power in range(levels)]
    partner = lax.switch(level, branches, updated)
    mixed_weights = ((updated + partner) * 0.5).astype(jnp.bfloat16)
    return (mixed_weights[None], new_moments[None])


def solution(mesh):
    return jax.shard_map(
        body,
        mesh=mesh,
        in_specs=(
            P(("replica", "fsdp"), None),
            P(("replica", "fsdp"), None),
            P("replica", "fsdp", None),
            P("replica", "fsdp", None),
            P(),
        ),
        out_specs=(P("replica", "fsdp", None), P("replica", "fsdp", None)),
        check_vma=False,
    )
```

profile of v0, /device:TPU:0, one launch (start us, length us, event | category | flops | bytes accessed | tf_op | source)
XLA Modules:
  0.0 194.2 jit_solution(16477069982003535401)
XLA Ops:
  7.2 0.0 all-gather.2.cloned.1.call-start
  7.2 0.7 all-gather.2.cloned.1.call-update
  7.9 2.7 %copy.11 = bf16[24,4,8,1024]{3,2,0,1:T(8,128)(2,1)} copy(bf16[24,4,8,1024]{3,2,1,0:T(8,128)(2,1)} %bitcast.20) | data formatting | bytes 3145728 | tf_op jit(solution)/shard_map/all_to_all | solution.py:20
  10.6 6.3 %all-to-all-start = ((bf16[192,4,1024]{2,0,1:T(8,128)(2,1)}), bf16[192,4,1024]{2,0,1:T(8,128)(2,1)S(1)}, u32[]{:S(2)}, u32[]{:S(2)}) async-start(bf16[192,4,1024]{2,0,1:T(8,128)(2,1)} %bitcast.17), calls=%async_computation | async-start | bytes 3145728 | tf_op jit(solution)/shard_map/all_to_all | solution.py:20
  17.6 58.7 %all-gather.2.cloned.1.call-done = bf16[768,1024]{1,0:T(8,128)(2,1)} async-done(((bf16[192,1024]{1,0:T(8,128)(2,1)}), bf16[768,1024]{1,0:T(8,128)(2,1)}) %all-gather.2.cloned.1.call-update) | async-done | bytes 1572880 | tf_op jit(solution)/shard_map/all_gather | solution.py:23
  76.3 2.9 %all-to-all-done = bf16[192,4,1024]{2,0,1:T(8,128)(2,1)S(1)} async-done(((bf16[192,4,1024]{2,0,1:T(8,128)(2,1)}), bf16[192,4,1024]{2,0,1:T(8,128)(2,1)S(1)}, u32[]{:S(2)}, u32[]{:S(2)}) %all-to-all-start) | async-done | bytes 1572896 | tf_op jit(solution)/shard_map/all_to_all | solution.py:20
  79.2 7.8 %convert_subtract_fusion = (f32[1024,1024]{1,0:T(8,128)S(1)}, f32[1024,1024]{1,0:T(8,128)}) fusion(bf16[1,1024,1024]{2,1,0:T(8,128)(2,1)} %param.10, bf16[768,1024]{1,0:T(8,128)(2,1)S(1)} %bitcast.18, bf16[768,1024]{1,0:T(8,128)(2,1)} %all-gather.2.cloned.1.call-done, f32[1,1024,1024]{2,1,0:T(8,128)} %param.11), kind=kOutput, calls=%fused_computation | convolution fusion | flops 1616904192 | bytes 17825792 | tf_op jit(solution)/shard_map/dot_general | solution.py:21
  87.0 0.0 copy-start
  87.0 1.9 %copy-done = f32[1024,1024]{1,0:T(8,128)} copy-done((f32[1024,1024]{1,0:T(8,128)}, f32[1024,1024]{1,0:T(8,128)S(1)}, u32[]{:S(2)}) %copy-start) | copy-done | bytes 4194328
  88.9 92.6 %conditional.1 = (f32[1024,1024]{1,0:T(8,128)}) conditional(s32[]{:T(128)} %clamp.3, f32[1024,1024]{1,0:T(8,128)S(1)} %get-tuple-element.9, f32[1024,1024]{1,0:T(8,128)S(1)} %get-tuple-element.9, f32[1024,1024]{1,0:T(8,128)S(1)} %get-tuple-element.9), branch_computations={%region_0.1_spmd, %region_1.2_spmd, %region_2.3_spmd} | conditional | bytes 16777264 | solution.py:34
  88.9 1.5 collective-permute-start.1
  90.4 91.1 %collective-permute-done.1 = f32[1024,1024]{1,0:T(8,128)} collective-permute-done((f32[1024,1024]{1,0:T(8,128)S(1)}, f32[1024,1024]{1,0:T(8,128)}, u32[]{:S(2)}, u32[]{:S(2)}) %collective-permute-start.1) | collective-permute-done | bytes 4194336 | tf_op jit(solution)/shard_map/cond/branch_1_fun/ppermute | solution.py:12
  181.5 5.9 %fusion = bf16[1,1024,1024]{2,1,0:T(8,128)(2,1)} fusion(f32[1024,1024]{1,0:T(8,128)} %copy-done, f32[1024,1024]{1,0:T(8,128)} %get-tuple-element.11), kind=kLoop, calls=%fused_computation.3 | loop fusion | flops 3145728 | bytes 10485760 | tf_op jit(solution)/shard_map/broadcast_in_dim | solution.py:36
Async XLA Ops:
  7.2 69.1 %all-gather.2.cloned.1.call-start = ((), (), s32[]{:S(2)}) async-start(), calls=%async_computation.1 | async-start | bytes 1966080 | tf_op jit(solution)/shard_map/all_gather | solution.py:23
  10.6 68.6 %all-to-all-start = ((bf16[192,4,1024]{2,0,1:T(8,128)(2,1)}), bf16[192,4,1024]{2,0,1:T(8,128)(2,1)S(1)}, u32[]{:S(2)}, u32[]{:S(2)}) async-start(bf16[192,4,1024]{2,0,1:T(8,128)(2,1)} %bitcast.17), calls=%async_computation | async-start | bytes 3145728 | tf_op jit(solution)/shard_map/all_to_all | solution.py:20
  87.0 1.9 %copy-start = (f32[1024,1024]{1,0:T(8,128)}, f32[1024,1024]{1,0:T(8,128)S(1)}, u32[]{:S(2)}) copy-start(f32[1024,1024]{1,0:T(8,128)S(1)} %get-tuple-element.9) | copy-start | bytes 12582916
  88.9 92.6 %collective-permute-start.1 = (f32[1024,1024]{1,0:T(8,128)S(1)}, f32[1024,1024]{1,0:T(8,128)}, u32[]{:S(2)}, u32[]{:S(2)}) collective-permute-start(f32[1024,1024]{1,0:T(8,128)S(1)} %param.1), channel_id=1, source_target_pairs={{24,0},{28,4},{0,8},{4,12},{8,16},{12,20},{16,24},{20,28},{25,1},{... | collective-permute-start | bytes 12582920 | tf_op jit(solution)/shard_map/cond/branch_1_fun/ppermute | solution.py:12
Sparse Core Ops, SparseCore 0:
  9.5 66.7 all-gather.1
where the time goes:
time: 194 us
  waiting for transfers between devices  153 us (79%)
  between operations  14.7 us (8%)
  starting transfers between devices  7.86 us (4%)
  matrix products  7.78 us (4%)
  other arithmetic  5.89 us (3%)
  local copies, waits for them, and re-layouts  4.65 us (2%)
    ppermute x1, waiting for transfers between devices, from_behind(): return lax.ppermute(block, axis, route)  91.1 us
    all_gather x1, waiting for transfers between devices, body(): lax.all_gather(grads_out, 'fsdp', axis=0, tiled=True)  58.7 us
    dot_general x1, matrix products, body(): lax.dot_general(features, lax.all_gather(grads_out, 'fsdp', axis=0, tiled...  7.78 us
    all_to_all x1, starting transfers between devices, body(): lax.all_to_all(tokens, 'fsdp', split_axis=1, concat_axis=0, tiled=True)  6.35 us
    broadcast_in_dim x1, other arithmetic, body(): return (mixed_weights[None], new_moments[None])  5.89 us
  transfers between devices with their start and end apart: 3, of which 3 were waited for; matrix products, arithmetic and copies ran while one was open for 1% of the time, Pallas kernels for 0%

commit v1 on v0

v1 whole, which is shorter than its diff:
```python
from functools import partial

import math
import jax
import jax.numpy as jnp
from jax import lax
from jax.sharding import PartitionSpec as P

SIZES = (1, 1, 1, 1)
FAR = "direct"


def ring(axis, reach):
    count = lax.axis_size(axis)
    return [(i, (i + reach) % count) for i in range(count)]


def after(value, *others):
    return lax.optimization_barrier((value, *others))[0]


def gather_line(block, axis):
    count = lax.axis_size(axis)
    me = lax.axis_index(axis)
    up, down = [block], [block]
    last = count - 1 if FAR == "direct" else count
    for k in range(1, last):
        up.append(lax.ppermute(up[-1], axis, [(i - 1, i) for i in range(k, count)]))
        down.append(lax.ppermute(down[-1], axis, [(i + 1, i) for i in range(count - k)]))
    if FAR == "direct":
        far = lax.ppermute(block, axis, [(0, count - 1), (count - 1, 0)])
        up.append(far)
        down.append(far)
    out = [block]
    for k in range(1, count):
        out.append(jnp.where(me >= k, up[k], down[count - k]))
    return out, [up[1], down[1]]


def gossip(reach, tokens, grads_out, weights, moments):
    shards = lax.axis_size("fsdp")
    me = lax.axis_index("fsdp")
    total_tokens = tokens.shape[0] * shards
    scale = jnp.float32(total_tokens ** (-0.5))
    width = tokens.shape[1] // shards
    limit = 1.0 + 36.0 * 0.05 * total_tokens ** 0.5
    wire = jnp.float32(2.0 ** math.floor(math.log2(60000.0 / limit)))
    unit = width // sum(SIZES)
    grads, hops = gather_line(grads_out, "fsdp")
    grads = jnp.concatenate(grads, 0)
    mixed, news, got = [], [], []
    at = 0
    for c, size in enumerate(SIZES):
        part = size * unit
        source = tokens
        if c == 1:
            source = after(tokens, *hops)
        if c > 1:
            source = after(tokens, *got[c - 2])
        pieces = [
            lax.dynamic_slice_in_dim(source, lax.rem(me + k, shards) * width + at, part, 1)
            for k in range(shards)
        ]
        feats = [pieces[0]]
        for k in range(1, shards):
            feats.append(lax.ppermute(pieces[k], "fsdp", ring("fsdp", k)))
        got.append(feats[1:])
        if c > 0:
            *feats, sent = lax.optimization_barrier((*feats, sent))
        feats = jnp.concatenate(feats, 0)
        rows = slice(at, at + part)
        gradient = lax.dot_general(feats, grads, (((0,), (0,)), ((), ())), preferred_element_type=jnp.float32)
        new = 0.9 * moments[0, rows] + gradient * scale
        updated = weights[0, rows].astype(jnp.float32) - 0.05 * new
        sent = (updated * wire).astype(jnp.float16)
        partner = lax.ppermute(sent, "replica", ring("replica", reach))
        mixed.append((updated, partner))
        news.append(new)
        at += part
    mixed = [((u + p.astype(jnp.float32) * (1.0 / wire)) * 0.5).astype(jnp.bfloat16) for u, p in mixed]
    return jnp.concatenate(mixed, 0)[None], jnp.concatenate(news, 0)[None]


def body(tokens, grads_out, weights, moments, step):
    levels = lax.axis_size("replica").bit_length() - 1
    level = step[0] % levels
    branches = [partial(gossip, 1 << power) for power in range(levels)]
    return lax.switch(level, branches, tokens, grads_out, weights, moments)


def solution(mesh):
    return jax.shard_map(
        body,
        mesh=mesh,
        in_specs=(
            P(("replica", "fsdp"), None),
            P(("replica", "fsdp"), None),
            P("replica", "fsdp", None),
            P("replica", "fsdp", None),
            P(),
        ),
        out_specs=(P("replica", "fsdp", None), P("replica", "fsdp", None)),
        check_vma=False,
    )
```

time: 194 us -> 116 us (0.60)
  waiting for transfers between devices: 153 us -> 58.8 us
  starting transfers between devices: 7.86 us -> 39.8 us
  between operations: 14.7 us -> 1.29 us
  matrix products: 7.78 us -> 4.2 us
    all_gather x1 -> x0, waiting for transfers between devices: 58.7 us -> none  [body(): lax.all_gather(grads_out, 'fsdp', axis=0, tiled=True)]
    ppermute x1 -> x21, starting transfers between devices: 1.48 us -> 39.8 us  [the longest x12 20.3 us: gossip(): feats.append(lax.ppermute(pieces[k], 'fsdp', ring('fsdp', k)))]
    ppermute x1 -> x21, waiting for transfers between devices: 91.1 us -> 58.8 us  [the longest x4 30.7 us: gossip(): partner = lax.ppermute(sent, 'replica', ring('replica', reach))]
    all_to_all x1 -> x0, starting transfers between devices: 6.35 us -> none  [body(): lax.all_to_all(tokens, 'fsdp', split_axis=1, concat_axis=0, tiled=True)]
    dynamic_slice x0 -> x4, local copies, waits for them, and re-layouts: none -> 5.07 us  [gossip(): lax.dynamic_slice_in_dim(source, lax.rem(me + k, shards) * width + at, pa...]
    dot_general x1 -> x4, matrix products: 7.78 us -> 4.2 us  [gossip(): lax.dot_general(feats, grads, (((0,), (0,)), ((), ())), preferred_element...]
    all_to_all x1 -> x0, waiting for transfers between devices: 2.88 us -> none  [body(): lax.all_to_all(tokens, 'fsdp', split_axis=1, concat_axis=0, tiled=True)]
    all_to_all x1 -> x0, local copies, waits for them, and re-layouts: 2.71 us -> none  [body(): lax.all_to_all(tokens, 'fsdp', split_axis=1, concat_axis=0, tiled=True)]
  transfers between devices with their start and end apart: 3 -> 21, of which waited for: 3 -> 9; matrix products, arithmetic and copies ran while one was open for 1% -> 10% of each run, Pallas kernels for 0% -> 0%
where the time goes in v1:
time: 116 us
  waiting for transfers between devices  58.8 us (51%)
  starting transfers between devices  39.8 us (34%)
  local copies, waits for them, and re-layouts  5.73 us (5%)
  other arithmetic  5.42 us (5%)
  matrix products  4.2 us (4%)
  between operations  1.29 us (1%)
    ppermute x4, waiting for transfers between devices, gossip(): partner = lax.ppermute(sent, 'replica', ring('replica', reach))  30.7 us
    ppermute x12, waiting for transfers between devices, gossip(): feats.append(lax.ppermute(pieces[k], 'fsdp', ring('fsdp', k)))  22.9 us
    ppermute x12, starting transfers between devices, gossip(): feats.append(lax.ppermute(pieces[k], 'fsdp', ring('fsdp', k)))  20.3 us
    ppermute x2, starting transfers between devices, gather_line(): up.append(lax.ppermute(up[-1], axis, [(i - 1, i) for i in range(k, count)]))  6.3 us
    ppermute x4, starting transfers between devices, gossip(): partner = lax.ppermute(sent, 'replica', ring('replica', reach))  6.1 us
    ppermute x2, waiting for transfers between devices, gather_line(): lax.ppermute(down[-1], axis, [(i + 1, i) for i in range(count - k)])  5.15 us
    dynamic_slice x4, local copies, waits for them, and re-layouts, gossip(): lax.dynamic_slice_in_dim(source, lax.rem(me + k, shards) * width + at, pa...  5.07 us
    ppermute x1, starting transfers between devices, gather_line(): far = lax.ppermute(block, axis, [(0, count - 1), (count - 1, 0)])  4.54 us
  transfers between devices with their start and end apart: 21, of which 9 were waited for; matrix products, arithmetic and copies ran while one was open for 10% of the time, Pallas kernels for 0%

profile of v1, /device:TPU:0, one launch (start us, length us, event | category | flops | bytes accessed | tf_op | source)
XLA Modules:
  0.0 115.5 jit_solution(16612511703159370002)
XLA Ops:
  1.3 114.2 %conditional.1 = (bf16[1,1024,1024]{2,1,0:T(8,128)(2,1)}, f32[1,1024,1024]{2,1,0:T(8,128)}) conditional(s32[]{:T(128)} %clamp.3, (bf16[1,1024,1024]{2,1,0:T(8,128)(2,1)}, f32[1,1024,1024]{2,1,0:T(8,128)}, bf16[192,4096]{1,0:T(8,128)(2,1)}, bf16[192,1024]{1,0:T(8,128)(2,1)}) %tuple.37, (bf16[1,1024,1024]{2,1,0:T(8,128)(2,1)}, ...), branch_computations={%region_0.1_spmd, %region_1.2_spmd, %region_2.3_spmd} | conditional | flops 1670971392 | bytes 98306088 | solution.py:88
  2.6 5.6 %collective-permute-start.24 = (bf16[192,1024]{1,0:T(8,128)(2,1)}, bf16[192,1024]{1,0:T(8,128)(2,1)S(1)}, u32[]{:S(2)}, u32[]{:S(2)}) collective-permute-start(bf16[192,1024]{1,0:T(8,128)(2,1)} %get-tuple-element.46), channel_id=1, source_target_pairs={{0,1},{1,2},{2,3},{4,5},{5,6},{6,7},{8,9},{9,10},{10,11},{12,13},{... | collective-permute-start | bytes 1179656 | tf_op jit(solution)/shard_map/cond/branch_1_fun/ppermute | solution.py:28
  8.3 1.9 %constant_dynamic-slice_fusion.31 = (bf16[192,256]{1,0:T(8,128)(2,1)S(1)}, bf16[192,256]{1,0:T(8,128)(2,1)S(1)}, bf16[192,256]{1,0:T(8,128)(2,1)}, bf16[192,256]{1,0:T(8,128)(2,1)S(1)}) fusion(bf16[192,4096]{1,0:T(8,128)(2,1)} %get-tuple-element.57, s32[]{:T(128)S(6)} %select_n.162, s32[]{:T(128)S(6)} %select_n.165, s32[]{:T(128)S(6)} %select_n.164, ...), kind=kLoop, calls=%fused_computation.143 | loop fusion | bytes 786448 | tf_op jit(solution)/shard_map/cond/branch_1_fun/dynamic_slice | solution.py:61
  10.1 1.8 %collective-permute-start.23 = (bf16[192,256]{1,0:T(8,128)(2,1)S(1)}, bf16[192,256]{1,0:T(8,128)(2,1)S(1)}, u32[]{:S(2)}, u32[]{:S(2)}) collective-permute-start(bf16[192,256]{1,0:T(8,128)(2,1)S(1)} %get-tuple-element.120), channel_id=1, source_target_pairs={{0,3},{1,0},{2,1},{3,2},{4,7},{5,4},{6,5},{7,6},{8,11},{9,8},{10,9... | collective-permute-start | bytes 294920 | tf_op jit(solution)/shard_map/cond/branch_1_fun/ppermute | solution.py:66
  12.0 4.5 %collective-permute-start.25 = (bf16[192,1024]{1,0:T(8,128)(2,1)}, bf16[192,1024]{1,0:T(8,128)(2,1)S(1)}, u32[]{:S(2)}, u32[]{:S(2)}) collective-permute-start(bf16[192,1024]{1,0:T(8,128)(2,1)} %get-tuple-element.46), channel_id=1, source_target_pairs={{0,3},{3,0},{4,7},{7,4},{8,11},{11,8},{12,15},{15,12},{16,19},{19,... | collective-permute-start | bytes 1179656 | tf_op jit(solution)/shard_map/cond/branch_1_fun/ppermute | solution.py:31
  16.6 3.4 %collective-permute-done.23 = bf16[192,256]{1,0:T(8,128)(2,1)S(1)} collective-permute-done((bf16[192,256]{1,0:T(8,128)(2,1)S(1)}, bf16[192,256]{1,0:T(8,128)(2,1)S(1)}, u32[]{:S(2)}, u32[]{:S(2)}) %collective-permute-start.23) | collective-permute-done | bytes 98336 | tf_op jit(solution)/shard_map/cond/branch_1_fun/ppermute | solution.py:66
  20.7 13.0 %collective-permute-done.22 = bf16[192,256]{1,0:T(8,128)(2,1)} collective-permute-done((bf16[192,256]{1,0:T(8,128)(2,1)}, bf16[192,256]{1,0:T(8,128)(2,1)}, u32[]{:S(2)}, u32[]{:S(2)}) %collective-permute-start.22) | collective-permute-done | bytes 98336 | tf_op jit(solution)/shard_map/cond/branch_1_fun/ppermute | solution.py:66
  35.9 3.5 %collective-permute-start.32 = (bf16[192,256]{1,0:T(8,128)(2,1)S(1)}, bf16[192,256]{1,0:T(8,128)(2,1)S(1)}, u32[]{:S(2)}, u32[]{:S(2)}) collective-permute-start(bf16[192,256]{1,0:T(8,128)(2,1)S(1)} %get-tuple-element.124), channel_id=1, source_target_pairs={{0,3},{1,0},{2,1},{3,2},{4,7},{5,4},{6,5},{7,6},{8,11},{9,8},{10,9... | collective-permute-start | bytes 294920 | tf_op jit(solution)/shard_map/cond/branch_1_fun/ppermute | solution.py:66
  39.7 1.9 %collective-permute-start.30 = (bf16[192,256]{1,0:T(8,128)(2,1)S(1)}, bf16[192,256]{1,0:T(8,128)(2,1)S(1)}, u32[]{:S(2)}, u32[]{:S(2)}) collective-permute-start(bf16[192,256]{1,0:T(8,128)(2,1)S(1)} %get-tuple-element.126), channel_id=1, source_target_pairs={{0,1},{1,2},{2,3},{3,0},{4,5},{5,6},{6,7},{7,4},{8,9},{9,10},{10,1... | collective-permute-start | bytes 294920 | tf_op jit(solution)/shard_map/cond/branch_1_fun/ppermute | solution.py:66
  43.7 2.6 %collective-permute-start.36 = (bf16[192,256]{1,0:T(8,128)(2,1)S(1)}, bf16[192,256]{1,0:T(8,128)(2,1)S(1)}, u32[]{:S(2)}, u32[]{:S(2)}) collective-permute-start(bf16[192,256]{1,0:T(8,128)(2,1)S(1)} %get-tuple-element.127), channel_id=1, source_target_pairs={{0,3},{1,0},{2,1},{3,2},{4,7},{5,4},{6,5},{7,6},{8,11},{9,8},{10,9... | collective-permute-start | bytes 294920 | tf_op jit(solution)/shard_map/cond/branch_1_fun/ppermute | solution.py:66
  46.4 3.9 %collective-permute-done.31 = bf16[192,256]{1,0:T(8,128)(2,1)S(1)} collective-permute-done((bf16[192,256]{1,0:T(8,128)(2,1)S(1)}, bf16[192,256]{1,0:T(8,128)(2,1)S(1)}, u32[]{:S(2)}, u32[]{:S(2)}) %collective-permute-start.31) | collective-permute-done | bytes 98336 | tf_op jit(solution)/shard_map/cond/branch_1_fun/ppermute | solution.py:66
  52.8 5.2 %collective-permute-done.28 = bf16[192,1024]{1,0:T(8,128)(2,1)S(1)} collective-permute-done((bf16[192,1024]{1,0:T(8,128)(2,1)S(1)}, bf16[192,1024]{1,0:T(8,128)(2,1)S(1)}, u32[]{:S(2)}, u32[]{:S(2)}) %collective-permute-start.28) | collective-permute-done | bytes 393248 | tf_op jit(solution)/shard_map/cond/branch_1_fun/ppermute | solution.py:29
  57.9 8.5 %collective-permute-start.39 = (bf16[192,256]{1,0:T(8,128)(2,1)S(1)}, bf16[192,256]{1,0:T(8,128)(2,1)S(1)}, u32[]{:S(2)}, u32[]{:S(2)}) collective-permute-start(bf16[192,256]{1,0:T(8,128)(2,1)S(1)} %get-tuple-element.132), channel_id=1, source_target_pairs={{0,2},{1,3},{2,0},{3,1},{4,6},{5,7},{6,4},{7,5},{8,10},{9,11},{10,... | collective-permute-start | bytes 294920 | tf_op jit(solution)/shard_map/cond/branch_1_fun/ppermute | solution.py:66
  66.5 1.9 %multiply_convert_fusion.15 = (f16[256,1024]{1,0:T(8,128)(2,1)S(1)}, f32[256,1024]{1,0:T(8,128)S(1)}) fusion(bf16[1,1024,1024]{2,1,0:T(8,128)(2,1)S(1)} %copy-done.1, bf16[192,1024]{1,0:T(8,128)(2,1)S(1)} %get-tuple-element.136, bf16[192,1024]{1,0:T(8,128)(2,1)S(1)} %broadcast_select_fusion.4, bf16[192,1024]{1,0:T(8,128)(2,1)S(1)} %get-tuple-element.135, ...), kind=kOutput, calls=%fused_computation.96 | convolution fusion | flops 412614656 | bytes 5111808 | tf_op jit(solution)/shard_map/cond/branch_1_fun/dot_general | solution.py:72
  69.3 1.6 %collective-permute-start.29 = (f16[256,1024]{1,0:T(8,128)(2,1)S(1)}, f16[256,1024]{1,0:T(8,128)(2,1)S(1)}, u32[]{:S(2)}, u32[]{:S(2)}) collective-permute-start(f16[256,1024]{1,0:T(8,128)(2,1)S(1)} %get-tuple-element.137), channel_id=1, source_target_pairs={{0,8},{4,12},{8,16},{12,20},{16,24},{20,28},{24,0},{28,4},{1,9},{5... | collective-permute-start | bytes 1572872 | tf_op jit(solution)/shard_map/cond/branch_1_fun/ppermute | solution.py:76
  70.8 1.5 %collective-permute-start.33 = (f16[256,1024]{1,0:T(8,128)(2,1)S(1)}, f16[256,1024]{1,0:T(8,128)(2,1)S(1)}, u32[]{:S(2)}, u32[]{:S(2)}) collective-permute-start(f16[256,1024]{1,0:T(8,128)(2,1)S(1)} %get-tuple-element.139), channel_id=1, source_target_pairs={{0,8},{4,12},{8,16},{12,20},{16,24},{20,28},{24,0},{28,4},{1,9},{5... | collective-permute-start | bytes 1572872 | tf_op jit(solution)/shard_map/cond/branch_1_fun/ppermute | solution.py:76
  73.1 2.5 %collective-permute-done.38 = bf16[192,256]{1,0:T(8,128)(2,1)S(1)} collective-permute-done((bf16[192,256]{1,0:T(8,128)(2,1)S(1)}, bf16[192,256]{1,0:T(8,128)(2,1)S(1)}, u32[]{:S(2)}, u32[]{:S(2)}) %collective-permute-start.38) | collective-permute-done | bytes 98336 | tf_op jit(solution)/shard_map/cond/branch_1_fun/ppermute | solution.py:66
  76.4 1.6 %collective-permute-start.41 = (f16[256,1024]{1,0:T(8,128)(2,1)S(1)}, f16[256,1024]{1,0:T(8,128)(2,1)S(1)}, u32[]{:S(2)}, u32[]{:S(2)}) collective-permute-start(f16[256,1024]{1,0:T(8,128)(2,1)S(1)} %get-tuple-element.143), channel_id=1, source_target_pairs={{0,8},{4,12},{8,16},{12,20},{16,24},{20,28},{24,0},{28,4},{1,9},{5... | collective-permute-start | bytes 1572872 | tf_op jit(solution)/shard_map/cond/branch_1_fun/ppermute | solution.py:76
  78.0 1.5 %collective-permute-start.37 = (f16[256,1024]{1,0:T(8,128)(2,1)S(1)}, f16[256,1024]{1,0:T(8,128)(2,1)S(1)}, u32[]{:S(2)}, u32[]{:S(2)}) collective-permute-start(f16[256,1024]{1,0:T(8,128)(2,1)S(1)} %get-tuple-element.141), channel_id=1, source_target_pairs={{0,8},{4,12},{8,16},{12,20},{16,24},{20,28},{24,0},{28,4},{1,9},{5... | collective-permute-start | bytes 1572872 | tf_op jit(solution)/shard_map/cond/branch_1_fun/ppermute | solution.py:76
  79.5 2.6 %maximum_bitcast_fusion.2 = f32[1,1024,1024]{2,1,0:T(8,128)} fusion(f32[256,1024]{1,0:T(8,128)S(1)} %get-tuple-element.144, f32[256,1024]{1,0:T(8,128)S(1)} %get-tuple-element.142, f32[256,1024]{1,0:T(8,128)S(1)} %get-tuple-element.140, f32[256,1024]{1,0:T(8,128)S(1)} %get-tuple-element.138), kind=kLoop, calls=%fused_computation.74 | loop fusion | flops 3145728 | bytes 8388608 | tf_op jit(solution)/shard_map/cond/branch_1_fun/broadcast_in_dim | solution.py:81
  82.1 2.9 %collective-permute-done.29 = f16[256,1024]{1,0:T(8,128)(2,1)S(1)} collective-permute-done((f16[256,1024]{1,0:T(8,128)(2,1)S(1)}, f16[256,1024]{1,0:T(8,128)(2,1)S(1)}, u32[]{:S(2)}, u32[]{:S(2)}) %collective-permute-start.29) | collective-permute-done | bytes 524320 | tf_op jit(solution)/shard_map/cond/branch_1_fun/ppermute | solution.py:76
  85.0 11.2 %collective-permute-done.33 = f16[256,1024]{1,0:T(8,128)(2,1)S(1)} collective-permute-done((f16[256,1024]{1,0:T(8,128)(2,1)S(1)}, f16[256,1024]{1,0:T(8,128)(2,1)S(1)}, u32[]{:S(2)}, u32[]{:S(2)}) %collective-permute-start.33) | collective-permute-done | bytes 524320 | tf_op jit(solution)/shard_map/cond/branch_1_fun/ppermute | solution.py:76
  96.3 10.9 %collective-permute-done.41 = f16[256,1024]{1,0:T(8,128)(2,1)S(1)} collective-permute-done((f16[256,1024]{1,0:T(8,128)(2,1)S(1)}, f16[256,1024]{1,0:T(8,128)(2,1)S(1)}, u32[]{:S(2)}, u32[]{:S(2)}) %collective-permute-start.41) | collective-permute-done | bytes 524320 | tf_op jit(solution)/shard_map/cond/branch_1_fun/ppermute | solution.py:76
  107.2 5.6 %collective-permute-done.37 = f16[256,1024]{1,0:T(8,128)(2,1)S(1)} collective-permute-done((f16[256,1024]{1,0:T(8,128)(2,1)S(1)}, f16[256,1024]{1,0:T(8,128)(2,1)S(1)}, u32[]{:S(2)}, u32[]{:S(2)}) %collective-permute-start.37) | collective-permute-done | bytes 524320 | tf_op jit(solution)/shard_map/cond/branch_1_fun/ppermute | solution.py:76
  (42 shorter events, 14.1 us)
Async XLA Ops:
  1.3 33.5 %collective-permute-start.27 = (bf16[192,1024]{1,0:T(8,128)(2,1)}, bf16[192,1024]{1,0:T(8,128)(2,1)S(1)}, u32[]{:S(2)}, u32[]{:S(2)}) collective-permute-start(bf16[192,1024]{1,0:T(8,128)(2,1)} %get-tuple-element.46), channel_id=1, source_target_pairs={{1,0},{2,1},{3,2},{5,4},{6,5},{7,6},{9,8},{10,9},{11,10},{13,12},{... | collective-permute-start | bytes 1179656 | tf_op jit(solution)/shard_map/cond/branch_1_fun/ppermute | solution.py:29
  2.6 32.2 %collective-permute-start.24 = (bf16[192,1024]{1,0:T(8,128)(2,1)}, bf16[192,1024]{1,0:T(8,128)(2,1)S(1)}, u32[]{:S(2)}, u32[]{:S(2)}) collective-permute-start(bf16[192,1024]{1,0:T(8,128)(2,1)} %get-tuple-element.46), channel_id=1, source_target_pairs={{0,1},{1,2},{2,3},{4,5},{5,6},{6,7},{8,9},{9,10},{10,11},{12,13},{... | collective-permute-start | bytes 1179656 | tf_op jit(solution)/shard_map/cond/branch_1_fun/ppermute | solution.py:28
  8.3 58.2 %copy-start.1 = (bf16[1,1024,1024]{2,1,0:T(8,128)(2,1)S(1)}, bf16[1,1024,1024]{2,1,0:T(8,128)(2,1)}, u32[]{:S(2)}) copy-start(bf16[1,1024,1024]{2,1,0:T(8,128)(2,1)} %get-tuple-element.43) | copy-start | bytes 6291460 | tf_op jit(solution)/shard_map/cond
  10.1 9.9 %collective-permute-start.23 = (bf16[192,256]{1,0:T(8,128)(2,1)S(1)}, bf16[192,256]{1,0:T(8,128)(2,1)S(1)}, u32[]{:S(2)}, u32[]{:S(2)}) collective-permute-start(bf16[192,256]{1,0:T(8,128)(2,1)S(1)} %get-tuple-element.120), channel_id=1, source_target_pairs={{0,3},{1,0},{2,1},{3,2},{4,7},{5,4},{6,5},{7,6},{8,11},{9,8},{10,9... | collective-permute-start | bytes 294920 | tf_op jit(solution)/shard_map/cond/branch_1_fun/ppermute | solution.py:66
  12.0 30.9 %collective-permute-start.25 = (bf16[192,1024]{1,0:T(8,128)(2,1)}, bf16[192,1024]{1,0:T(8,128)(2,1)S(1)}, u32[]{:S(2)}, u32[]{:S(2)}) collective-permute-start(bf16[192,1024]{1,0:T(8,128)(2,1)} %get-tuple-element.46), channel_id=1, source_target_pairs={{0,3},{3,0},{4,7},{7,4},{8,11},{11,8},{12,15},{15,12},{16,19},{19,... | collective-permute-start | bytes 1179656 | tf_op jit(solution)/shard_map/cond/branch_1_fun/ppermute | solution.py:31
  16.5 17.2 %collective-permute-start.22 = (bf16[192,256]{1,0:T(8,128)(2,1)}, bf16[192,256]{1,0:T(8,128)(2,1)}, u32[]{:S(2)}, u32[]{:S(2)}) collective-permute-start(bf16[192,256]{1,0:T(8,128)(2,1)} %get-tuple-element.121), channel_id=1, source_target_pairs={{0,2},{1,3},{2,0},{3,1},{4,6},{5,7},{6,4},{7,5},{8,10},{9,11},{10,... | collective-permute-start | bytes 294920 | tf_op jit(solution)/shard_map/cond/branch_1_fun/ppermute | solution.py:66
  20.7 13.0 %collective-permute-start.21 = (bf16[192,256]{1,0:T(8,128)(2,1)S(1)}, bf16[192,256]{1,0:T(8,128)(2,1)}, u32[]{:S(2)}, u32[]{:S(2)}) collective-permute-start(bf16[192,256]{1,0:T(8,128)(2,1)S(1)} %get-tuple-element.122), channel_id=1, source_target_pairs={{0,1},{1,2},{2,3},{3,0},{4,5},{5,6},{6,7},{7,4},{8,9},{9,10},{10,1... | collective-permute-start | bytes 294920 | tf_op jit(solution)/shard_map/cond/branch_1_fun/ppermute | solution.py:66
  20.7 45.8 %copy-start.4 = (f32[1,1024,1024]{2,1,0:T(8,128)S(1)}, f32[1,1024,1024]{2,1,0:T(8,128)}, u32[]{:S(2)}) copy-start(f32[1,1024,1024]{2,1,0:T(8,128)} %get-tuple-element.44) | copy-start | bytes 12582916 | tf_op jit(solution)/shard_map/cond
  20.7 45.8 %copy-start.12 = (bf16[192,256]{1,0:T(8,128)(2,1)S(1)}, bf16[192,256]{1,0:T(8,128)(2,1)}, u32[]{:S(2)}) copy-start(bf16[192,256]{1,0:T(8,128)(2,1)} %copy-done.11) | copy-start | bytes 294916 | tf_op jit(solution)/shard_map/cond
  35.9 7.8 %collective-permute-start.32 = (bf16[192,256]{1,0:T(8,128)(2,1)S(1)}, bf16[192,256]{1,0:T(8,128)(2,1)S(1)}, u32[]{:S(2)}, u32[]{:S(2)}) collective-permute-start(bf16[192,256]{1,0:T(8,128)(2,1)S(1)} %get-tuple-element.124), channel_id=1, source_target_pairs={{0,3},{1,0},{2,1},{3,2},{4,7},{5,4},{6,5},{7,6},{8,11},{9,8},{10,9... | collective-permute-start | bytes 294920 | tf_op jit(solution)/shard_map/cond/branch_1_fun/ppermute | solution.py:66
  39.5 10.8 %collective-permute-start.31 = (bf16[192,256]{1,0:T(8,128)(2,1)S(1)}, bf16[192,256]{1,0:T(8,128)(2,1)S(1)}, u32[]{:S(2)}, u32[]{:S(2)}) collective-permute-start(bf16[192,256]{1,0:T(8,128)(2,1)S(1)} %get-tuple-element.125), channel_id=1, source_target_pairs={{0,2},{1,3},{2,0},{3,1},{4,6},{5,7},{6,4},{7,5},{8,10},{9,11},{10,... | collective-permute-start | bytes 294920 | tf_op jit(solution)/shard_map/cond/branch_1_fun/ppermute | solution.py:66
  39.7 10.8 %collective-permute-start.30 = (bf16[192,256]{1,0:T(8,128)(2,1)S(1)}, bf16[192,256]{1,0:T(8,128)(2,1)S(1)}, u32[]{:S(2)}, u32[]{:S(2)}) collective-permute-start(bf16[192,256]{1,0:T(8,128)(2,1)S(1)} %get-tuple-element.126), channel_id=1, source_target_pairs={{0,1},{1,2},{2,3},{3,0},{4,5},{5,6},{6,7},{7,4},{8,9},{9,10},{10,1... | collective-permute-start | bytes 294920 | tf_op jit(solution)/shard_map/cond/branch_1_fun/ppermute | solution.py:66
  41.6 16.3 %collective-permute-start.28 = (bf16[192,1024]{1,0:T(8,128)(2,1)S(1)}, bf16[192,1024]{1,0:T(8,128)(2,1)S(1)}, u32[]{:S(2)}, u32[]{:S(2)}) collective-permute-start(bf16[192,1024]{1,0:T(8,128)(2,1)S(1)} %collective-permute-done.27), channel_id=1, source_target_pairs={{1,0},{2,1},{5,4},{6,5},{9,8},{10,9},{13,12},{14,13},{17,16},{18,1... | collective-permute-start | bytes 1179656 | tf_op jit(solution)/shard_map/cond/branch_1_fun/ppermute | solution.py:29
  42.9 15.0 %collective-permute-start.26 = (bf16[192,1024]{1,0:T(8,128)(2,1)S(1)}, bf16[192,1024]{1,0:T(8,128)(2,1)S(1)}, u32[]{:S(2)}, u32[]{:S(2)}) collective-permute-start(bf16[192,1024]{1,0:T(8,128)(2,1)S(1)} %collective-permute-done.24), channel_id=1, source_target_pairs={{1,2},{2,3},{5,6},{6,7},{9,10},{10,11},{13,14},{14,15},{17,18},{18... | collective-permute-start | bytes 1179656 | tf_op jit(solution)/shard_map/cond/branch_1_fun/ppermute | solution.py:28
  43.7 25.5 %collective-permute-start.36 = (bf16[192,256]{1,0:T(8,128)(2,1)S(1)}, bf16[192,256]{1,0:T(8,128)(2,1)S(1)}, u32[]{:S(2)}, u32[]{:S(2)}) collective-permute-start(bf16[192,256]{1,0:T(8,128)(2,1)S(1)} %get-tuple-element.127), channel_id=1, source_target_pairs={{0,3},{1,0},{2,1},{3,2},{4,7},{5,4},{6,5},{7,6},{8,11},{9,8},{10,9... | collective-permute-start | bytes 294920 | tf_op jit(solution)/shard_map/cond/branch_1_fun/ppermute | solution.py:66
  50.2 19.0 %collective-permute-start.35 = (bf16[192,256]{1,0:T(8,128)(2,1)S(1)}, bf16[192,256]{1,0:T(8,128)(2,1)S(1)}, u32[]{:S(2)}, u32[]{:S(2)}) collective-permute-start(bf16[192,256]{1,0:T(8,128)(2,1)S(1)} %get-tuple-element.128), channel_id=1, source_target_pairs={{0,2},{1,3},{2,0},{3,1},{4,6},{5,7},{6,4},{7,5},{8,10},{9,11},{10,... | collective-permute-start | bytes 294920 | tf_op jit(solution)/shard_map/cond/branch_1_fun/ppermute | solution.py:66
  50.5 20.4 %collective-permute-start.34 = (bf16[192,256]{1,0:T(8,128)(2,1)S(1)}, bf16[192,256]{1,0:T(8,128)(2,1)S(1)}, u32[]{:S(2)}, u32[]{:S(2)}) collective-permute-start(bf16[192,256]{1,0:T(8,128)(2,1)S(1)} %get-tuple-element.129), channel_id=1, source_target_pairs={{0,1},{1,2},{2,3},{3,0},{4,5},{5,6},{6,7},{7,4},{8,9},{9,10},{10,1... | collective-permute-start | bytes 294920 | tf_op jit(solution)/shard_map/cond/branch_1_fun/ppermute | solution.py:66
  57.9 15.2 %collective-permute-start.40 = (bf16[192,256]{1,0:T(8,128)(2,1)S(1)}, bf16[192,256]{1,0:T(8,128)(2,1)S(1)}, u32[]{:S(2)}, u32[]{:S(2)}) collective-permute-start(bf16[192,256]{1,0:T(8,128)(2,1)S(1)} %get-tuple-element.131), channel_id=1, source_target_pairs={{0,3},{1,0},{2,1},{3,2},{4,7},{5,4},{6,5},{7,6},{8,11},{9,8},{10,9... | collective-permute-start | bytes 294920 | tf_op jit(solution)/shard_map/cond/branch_1_fun/ppermute | solution.py:66
  57.9 15.2 %collective-permute-start.39 = (bf16[192,256]{1,0:T(8,128)(2,1)S(1)}, bf16[192,256]{1,0:T(8,128)(2,1)S(1)}, u32[]{:S(2)}, u32[]{:S(2)}) collective-permute-start(bf16[192,256]{1,0:T(8,128)(2,1)S(1)} %get-tuple-element.132), channel_id=1, source_target_pairs={{0,2},{1,3},{2,0},{3,1},{4,6},{5,7},{6,4},{7,5},{8,10},{9,11},{10,... | collective-permute-start | bytes 294920 | tf_op jit(solution)/shard_map/cond/branch_1_fun/ppermute | solution.py:66
  69.2 6.5 %collective-permute-start.38 = (bf16[192,256]{1,0:T(8,128)(2,1)S(1)}, bf16[192,256]{1,0:T(8,128)(2,1)S(1)}, u32[]{:S(2)}, u32[]{:S(2)}) collective-permute-start(bf16[192,256]{1,0:T(8,128)(2,1)S(1)} %get-tuple-element.133), channel_id=1, source_target_pairs={{0,1},{1,2},{2,3},{3,0},{4,5},{5,6},{6,7},{7,4},{8,9},{9,10},{10,1... | collective-permute-start | bytes 294920 | tf_op jit(solution)/shard_map/cond/branch_1_fun/ppermute | solution.py:66
  69.3 15.7 %collective-permute-start.29 = (f16[256,1024]{1,0:T(8,128)(2,1)S(1)}, f16[256,1024]{1,0:T(8,128)(2,1)S(1)}, u32[]{:S(2)}, u32[]{:S(2)}) collective-permute-start(f16[256,1024]{1,0:T(8,128)(2,1)S(1)} %get-tuple-element.137), channel_id=1, source_target_pairs={{0,8},{4,12},{8,16},{12,20},{16,24},{20,28},{24,0},{28,4},{1,9},{5... | collective-permute-start | bytes 1572872 | tf_op jit(solution)/shard_map/cond/branch_1_fun/ppermute | solution.py:76
  70.8 25.4 %collective-permute-start.33 = (f16[256,1024]{1,0:T(8,128)(2,1)S(1)}, f16[256,1024]{1,0:T(8,128)(2,1)S(1)}, u32[]{:S(2)}, u32[]{:S(2)}) collective-permute-start(f16[256,1024]{1,0:T(8,128)(2,1)S(1)} %get-tuple-element.139), channel_id=1, source_target_pairs={{0,8},{4,12},{8,16},{12,20},{16,24},{20,28},{24,0},{28,4},{1,9},{5... | collective-permute-start | bytes 1572872 | tf_op jit(solution)/shard_map/cond/branch_1_fun/ppermute | solution.py:76
  76.4 30.7 %collective-permute-start.41 = (f16[256,1024]{1,0:T(8,128)(2,1)S(1)}, f16[256,1024]{1,0:T(8,128)(2,1)S(1)}, u32[]{:S(2)}, u32[]{:S(2)}) collective-permute-start(f16[256,1024]{1,0:T(8,128)(2,1)S(1)} %get-tuple-element.143), channel_id=1, source_target_pairs={{0,8},{4,12},{8,16},{12,20},{16,24},{20,28},{24,0},{28,4},{1,9},{5... | collective-permute-start | bytes 1572872 | tf_op jit(solution)/shard_map/cond/branch_1_fun/ppermute | solution.py:76
  78.0 34.8 %collective-permute-start.37 = (f16[256,1024]{1,0:T(8,128)(2,1)S(1)}, f16[256,1024]{1,0:T(8,128)(2,1)S(1)}, u32[]{:S(2)}, u32[]{:S(2)}) collective-permute-start(f16[256,1024]{1,0:T(8,128)(2,1)S(1)} %get-tuple-element.141), channel_id=1, source_target_pairs={{0,8},{4,12},{8,16},{12,20},{16,24},{20,28},{24,0},{28,4},{1,9},{5... | collective-permute-start | bytes 1572872 | tf_op jit(solution)/shard_map/cond/branch_1_fun/ppermute | solution.py:76
  (2 other events, 2.6 us)

commit v2 on v1

v2 whole, which is shorter than its diff:
```python
from functools import partial

import math
import jax
import jax.numpy as jnp
from jax import lax
from jax.sharding import PartitionSpec as P

CUT = 4
SIZES = (1, 1, 1, 1)


def ring(axis, reach):
    count = lax.axis_size(axis)
    return [(i, (i + reach) % count) for i in range(count)]


def across(axis, flip):
    return [(i, i ^ flip) for i in range(lax.axis_size(axis))]


def after(value, *others):
    return lax.optimization_barrier((value, *others))[0]


def gather(block, axis):
    count = lax.axis_size(axis)
    blocks = {0: block}
    for flip in sorted(range(1, count), key=lambda f: (f.bit_count(), -f)):
        low = flip & -flip
        blocks[flip] = lax.ppermute(blocks[flip - low], axis, across(axis, low))
    return [blocks[flip] for flip in range(count)]


def gossip(reach, tokens, grads_out, weights, moments):
    shards = lax.axis_size("fsdp")
    me = lax.axis_index("fsdp")
    total_tokens = tokens.shape[0] * shards
    scale = jnp.float32(total_tokens ** (-0.5))
    width = tokens.shape[1] // shards
    limit = 1.0 + 36.0 * 0.05 * total_tokens ** 0.5
    wire = jnp.float32(2.0 ** math.floor(math.log2(60000.0 / limit)))
    unit = width // sum(SIZES)
    columns = grads_out.shape[1]
    half = columns * CUT // 8
    far = shards // 2

    left = lax.slice_in_dim(grads_out, 0, half, axis=1)
    left = gather(left, "fsdp")
    right = lax.slice_in_dim(after(grads_out, left[far]), half, columns, axis=1)
    right = gather(right, "fsdp")

    def block(feats, grads, rows, cols):
        gradient = lax.dot_general(feats, grads, (((0,), (0,)), ((), ())), preferred_element_type=jnp.float32)
        new = 0.9 * moments[0, rows, cols] + gradient * scale
        updated = weights[0, rows, cols].astype(jnp.float32) - 0.05 * new
        sent = (updated * wire).astype(jnp.float16)
        return new, updated, sent

    def send(sent):
        return lax.ppermute(sent, "replica", ring("replica", reach))

    done, got = [], []
    at = 0
    for c, size in enumerate(SIZES):
        part = size * unit
        source = tokens
        if c == 1:
            source = after(tokens, left[far])
        if c == 2:
            source = after(tokens, left[-1], *got[0])
        if c > 2:
            source = after(tokens, *got[c - 3])
        pieces = [lax.dynamic_slice_in_dim(source, (me ^ k) * width + at, part, 1) for k in range(shards)]
        feats = [pieces[0]]
        for k in range(1, shards):
            feats.append(lax.ppermute(pieces[k], "fsdp", across("fsdp", k)))
        got.append(feats[1:])
        if c > 0:
            *feats, sent = lax.optimization_barrier((*feats, sent))
        feats = jnp.concatenate(feats, 0)
        rows = slice(at, at + part)
        if c == 0:
            new, updated, sent = block(feats, jnp.concatenate(left, 0), rows, slice(0, half))
            done.append((at, 0, new, updated, send(sent)))
            right[-1], feats, sent = lax.optimization_barrier((right[-1], feats, sent))
            new, updated, sent = block(feats, jnp.concatenate(right, 0), rows, slice(half, columns))
            done.append((at, half, new, updated, send(sent)))
            grads = jnp.concatenate([jnp.concatenate([a, b], 1) for a, b in zip(left, right)], 0)
        else:
            new, updated, sent = block(feats, grads, rows, slice(None))
            done.append((at, 0, new, updated, send(sent)))
        at += part
    out = jnp.zeros(weights.shape[1:], weights.dtype)
    new_moments = jnp.zeros(moments.shape[1:], moments.dtype)
    for row, col, new, updated, partner in done:
        mixed = ((updated + partner.astype(jnp.float32) * (1.0 / wire)) * 0.5).astype(jnp.bfloat16)
        out = lax.dynamic_update_slice(out, mixed, (row, col))
        new_moments = lax.dynamic_update_slice(new_moments, new, (row, col))
    return out[None], new_moments[None]


def body(tokens, grads_out, weights, moments, step):
    levels = lax.axis_size("replica").bit_length() - 1
    level = step[0] % levels
    branches = [partial(gossip, 1 << power) for power in range(levels)]
    return lax.switch(level, branches, tokens, grads_out, weights, moments)


def solution(mesh):
    return jax.shard_map(
        body,
        mesh=mesh,
        in_specs=(
            P(("replica", "fsdp"), None),
            P(("replica", "fsdp"), None),
            P("replica", "fsdp", None),
            P("replica", "fsdp", None),
            P(),
        ),
        out_specs=(P("replica", "fsdp", None), P("replica", "fsdp", None)),
        check_vma=False,
    )
```

time: 116 us -> 110 us (0.948)
  starting transfers between devices: 39.8 us -> 33.7 us
  other arithmetic: 5.42 us -> 1.31 us
  matrix products: 4.2 us -> 7.47 us
  local copies, waits for them, and re-layouts: 5.73 us -> 7.68 us
    ppermute x21 -> x23, starting transfers between devices: 39.8 us -> 33.7 us  [the longest x12 20.3 us: gossip(): feats.append(lax.ppermute(pieces[k], 'fsdp', across('fsdp', k)))]
    broadcast_in_dim x2 -> x0, other arithmetic: 4.09 us -> none  [gossip(): return (jnp.concatenate(mixed, 0)[None], jnp.concatenate(news, 0)[None])]
    dot_general x4 -> x5, matrix products: 4.2 us -> 7.47 us  [block(): lax.dot_general(feats, grads, (((0,), (0,)), ((), ())), preferred_element...]
    ppermute x21 -> x23, waiting for transfers between devices: 58.8 us -> 57.9 us  [the longest x5 31.8 us: send(): return lax.ppermute(sent, 'replica', ring('replica', reach))]
  transfers between devices with their start and end apart: 21 -> 23, of which waited for: 9 -> 11; matrix products, arithmetic and copies ran while one was open for 10% -> 12% of each run, Pallas kernels for 0% -> 0%
where the time goes in v2:
time: 110 us
  waiting for transfers between devices  57.9 us (53%)
  starting transfers between devices  33.7 us (31%)
  local copies, waits for them, and re-layouts  7.68 us (7%)
  matrix products  7.47 us (7%)
  other arithmetic  1.31 us (1%)
  between operations  1.29 us (1%)
    ppermute x5, waiting for transfers between devices, send(): return lax.ppermute(sent, 'replica', ring('replica', reach))  31.8 us
    ppermute x12, starting transfers between devices, gossip(): feats.append(lax.ppermute(pieces[k], 'fsdp', across('fsdp', k)))  20.3 us
    ppermute x6, waiting for transfers between devices, gather(): blocks[flip] = lax.ppermute(blocks[flip - low], axis, across(axis, low))  14.2 us
    ppermute x12, waiting for transfers between devices, gossip(): feats.append(lax.ppermute(pieces[k], 'fsdp', across('fsdp', k)))  11.9 us
    dot_general x5, matrix products, block(): lax.dot_general(feats, grads, (((0,), (0,)), ((), ())), preferred_element...  7.47 us
    ppermute x6, starting transfers between devices, gather(): blocks[flip] = lax.ppermute(blocks[flip - low], axis, across(axis, low))  6.86 us
    ppermute x5, starting transfers between devices, send(): return lax.ppermute(sent, 'replica', ring('replica', reach))  6.55 us
    dynamic_slice x4, local copies, waits for them, and re-layouts, gossip(): lax.dynamic_slice_in_dim(source, (me ^ k) * width + at, part, 1)  4.32 us
  transfers between devices with their start and end apart: 23, of which 11 were waited for; matrix products, arithmetic and copies ran while one was open for 12% of the time, Pallas kernels for 0%

profile of v2, /device:TPU:0, one launch (start us, length us, event | category | flops | bytes accessed | tf_op | source)
XLA Modules:
  0.0 109.6 jit_solution(14667354726104620996)
XLA Ops:
  1.3 108.3 %conditional.1 = (bf16[1,1024,1024]{2,1,0:T(8,128)(2,1)}, f32[1,1024,1024]{2,1,0:T(8,128)}) conditional(s32[]{:T(128)} %clamp.3, (bf16[1,1024,1024]{2,1,0:T(8,128)(2,1)}, f32[1,1024,1024]{2,1,0:T(8,128)}, bf16[192,4096]{1,0:T(8,128)(2,1)}, bf16[192,1024]{1,0:T(8,128)(2,1)}) %tuple.43, (bf16[1,1024,1024]{2,1,0:T(8,128)(2,1)}, ...), branch_computations={%region_0.1_spmd, %region_1.2_spmd, %region_2.3_spmd} | conditional | flops 1679294464 | bytes 120194936 | solution.py:107
  2.5 5.1 %collective-permute-start.25 = (bf16[192,256]{1,0:T(8,128)(2,1)S(1)}, bf16[192,256]{1,0:T(8,128)(2,1)S(1)}, u32[]{:S(2)}, u32[]{:S(2)}) collective-permute-start(bf16[192,256]{1,0:T(8,128)(2,1)S(1)} %get-tuple-element.137), channel_id=1, source_target_pairs={{0,3},{1,2},{2,1},{3,0},{4,7},{5,6},{6,5},{7,4},{8,11},{9,10},{10,... | collective-permute-start | bytes 294920 | tf_op jit(solution)/shard_map/cond/branch_1_fun/ppermute | solution.py:77
  9.2 2.4 %collective-permute-start.27 = (bf16[192,512]{1,0:T(8,128)(2,1)S(1)}, bf16[192,512]{1,0:T(8,128)(2,1)}, u32[]{:S(2)}, u32[]{:S(2)}) collective-permute-start(bf16[192,512]{1,0:T(8,128)(2,1)S(1)} %slice.86), channel_id=1, source_target_pairs={{0,2},{1,3},{2,0},{3,1},{4,6},{5,7},{6,4},{7,5},{8,10},{9,11},{10,... | collective-permute-start | bytes 589832 | tf_op jit(solution)/shard_map/cond/branch_1_fun/ppermute | solution.py:31
  11.6 2.0 %collective-permute-start.26 = (bf16[192,512]{1,0:T(8,128)(2,1)S(1)}, bf16[192,512]{1,0:T(8,128)(2,1)}, u32[]{:S(2)}, u32[]{:S(2)}) collective-permute-start(bf16[192,512]{1,0:T(8,128)(2,1)S(1)} %slice.86), channel_id=1, source_target_pairs={{0,1},{1,0},{2,3},{3,2},{4,5},{5,4},{6,7},{7,6},{8,9},{9,8},{10,11... | collective-permute-start | bytes 589832 | tf_op jit(solution)/shard_map/cond/branch_1_fun/ppermute | solution.py:31
  13.6 7.5 %collective-permute-done.24 = bf16[192,256]{1,0:T(8,128)(2,1)S(1)} collective-permute-done((bf16[192,256]{1,0:T(8,128)(2,1)S(1)}, bf16[192,256]{1,0:T(8,128)(2,1)S(1)}, u32[]{:S(2)}, u32[]{:S(2)}) %collective-permute-start.24) | collective-permute-done | bytes 98336 | tf_op jit(solution)/shard_map/cond/branch_1_fun/ppermute | solution.py:77
  22.2 3.3 %collective-permute-start.43 = (bf16[192,256]{1,0:T(8,128)(2,1)S(1)}, bf16[192,256]{1,0:T(8,128)(2,1)S(1)}, u32[]{:S(2)}, u32[]{:S(2)}) collective-permute-start(bf16[192,256]{1,0:T(8,128)(2,1)S(1)} %get-tuple-element.125), channel_id=1, source_target_pairs={{0,2},{1,3},{2,0},{3,1},{4,6},{5,7},{6,4},{7,5},{8,10},{9,11},{10,... | collective-permute-start | bytes 294920 | tf_op jit(solution)/shard_map/cond/branch_1_fun/ppermute | solution.py:77
  26.6 2.4 %collective-permute-start.30 = (bf16[192,512]{1,0:T(8,128)(2,1)S(1)}, bf16[192,512]{1,0:T(8,128)(2,1)S(1)}, u32[]{:S(2)}, u32[]{:S(2)}) collective-permute-start(bf16[192,512]{1,0:T(8,128)(2,1)S(1)} %slice.89), channel_id=1, source_target_pairs={{0,2},{1,3},{2,0},{3,1},{4,6},{5,7},{6,4},{7,5},{8,10},{9,11},{10,... | collective-permute-start | bytes 589832 | tf_op jit(solution)/shard_map/cond/branch_1_fun/ppermute | solution.py:31
  30.1 6.4 %collective-permute-done.28 = bf16[192,512]{1,0:T(8,128)(2,1)S(1)} collective-permute-done((bf16[192,512]{1,0:T(8,128)(2,1)}, bf16[192,512]{1,0:T(8,128)(2,1)S(1)}, u32[]{:S(2)}, u32[]{:S(2)}) %collective-permute-start.28) | collective-permute-done | bytes 196640 | tf_op jit(solution)/shard_map/cond/branch_1_fun/ppermute | solution.py:31
  37.6 2.1 %collective-permute-start.34 = (bf16[192,256]{1,0:T(8,128)(2,1)S(1)}, bf16[192,256]{1,0:T(8,128)(2,1)S(1)}, u32[]{:S(2)}, u32[]{:S(2)}) collective-permute-start(bf16[192,256]{1,0:T(8,128)(2,1)S(1)} %get-tuple-element.134), channel_id=1, source_target_pairs={{0,1},{1,0},{2,3},{3,2},{4,5},{5,4},{6,7},{7,6},{8,9},{9,8},{10,11... | collective-permute-start | bytes 294920 | tf_op jit(solution)/shard_map/cond/branch_1_fun/ppermute | solution.py:77
  42.0 6.7 %collective-permute-done.31 = bf16[192,512]{1,0:T(8,128)(2,1)S(1)} collective-permute-done((bf16[192,512]{1,0:T(8,128)(2,1)S(1)}, bf16[192,512]{1,0:T(8,128)(2,1)S(1)}, u32[]{:S(2)}, u32[]{:S(2)}) %collective-permute-start.31) | collective-permute-done | bytes 196640 | tf_op jit(solution)/shard_map/cond/branch_1_fun/ppermute | solution.py:31
  51.3 5.7 %collective-permute-done.29 = f16[256,512]{1,0:T(8,128)(2,1)S(1)} collective-permute-done((f16[256,512]{1,0:T(8,128)(2,1)S(1)}, f16[256,512]{1,0:T(8,128)(2,1)S(1)}, u32[]{:S(2)}, u32[]{:S(2)}) %collective-permute-start.29) | collective-permute-done | bytes 262176 | tf_op jit(solution)/shard_map/cond/branch_1_fun/ppermute | solution.py:61
  57.0 1.7 %collective-permute-start.36 = (bf16[192,256]{1,0:T(8,128)(2,1)S(1)}, bf16[192,256]{1,0:T(8,128)(2,1)S(1)}, u32[]{:S(2)}, u32[]{:S(2)}) collective-permute-start(bf16[192,256]{1,0:T(8,128)(2,1)S(1)} %get-tuple-element.132), channel_id=1, source_target_pairs={{0,3},{1,2},{2,1},{3,0},{4,7},{5,6},{6,5},{7,4},{8,11},{9,10},{10,... | collective-permute-start | bytes 294920 | tf_op jit(solution)/shard_map/cond/branch_1_fun/ppermute | solution.py:77
  59.8 1.9 %collective-permute-start.39 = (bf16[192,256]{1,0:T(8,128)(2,1)S(1)}, bf16[192,256]{1,0:T(8,128)(2,1)S(1)}, u32[]{:S(2)}, u32[]{:S(2)}) collective-permute-start(bf16[192,256]{1,0:T(8,128)(2,1)S(1)} %get-tuple-element.129), channel_id=1, source_target_pairs={{0,2},{1,3},{2,0},{3,1},{4,6},{5,7},{6,4},{7,5},{8,10},{9,11},{10,... | collective-permute-start | bytes 294920 | tf_op jit(solution)/shard_map/cond/branch_1_fun/ppermute | solution.py:77
  61.8 1.8 %collective-permute-done.36 = bf16[192,256]{1,0:T(8,128)(2,1)S(1)} collective-permute-done((bf16[192,256]{1,0:T(8,128)(2,1)S(1)}, bf16[192,256]{1,0:T(8,128)(2,1)S(1)}, u32[]{:S(2)}, u32[]{:S(2)}) %collective-permute-start.36) | collective-permute-done | bytes 98336 | tf_op jit(solution)/shard_map/cond/branch_1_fun/ppermute | solution.py:77
  63.5 2.0 %collective-permute-start.40 = (bf16[192,256]{1,0:T(8,128)(2,1)S(1)}, bf16[192,256]{1,0:T(8,128)(2,1)S(1)}, u32[]{:S(2)}, u32[]{:S(2)}) collective-permute-start(bf16[192,256]{1,0:T(8,128)(2,1)S(1)} %get-tuple-element.128), channel_id=1, source_target_pairs={{0,3},{1,2},{2,1},{3,0},{4,7},{5,6},{6,5},{7,4},{8,11},{9,10},{10,... | collective-permute-start | bytes 294920 | tf_op jit(solution)/shard_map/cond/branch_1_fun/ppermute | solution.py:77
  65.5 1.8 %multiply_convert_fusion.15 = (f16[256,1024]{1,0:T(8,128)(2,1)S(1)}, f32[256,1024]{1,0:T(8,128)S(1)}) fusion(bf16[1,1024,1024]{2,1,0:T(8,128)(2,1)S(1)} %copy-done.1, bf16[192,512]{1,0:T(8,128)(2,1)S(1)} %collective-permute-done.31, bf16[192,512]{1,0:T(8,128)(2,1)S(1)} %collective-permute-done.28, bf16[192,512]{1,0:T(8,128)(2,1)S(1)} %collective-permute-done.30, ...), kind=kOutput, calls=%fused_computation.121 | convolution fusion | flops 418906112 | bytes 5111808 | tf_op jit(solution)/shard_map/cond/branch_1_fun/dot_general | solution.py:54
  67.3 1.9 %collective-permute-start.44 = (bf16[192,256]{1,0:T(8,128)(2,1)S(1)}, bf16[192,256]{1,0:T(8,128)(2,1)S(1)}, u32[]{:S(2)}, u32[]{:S(2)}) collective-permute-start(bf16[192,256]{1,0:T(8,128)(2,1)S(1)} %get-tuple-element.124), channel_id=1, source_target_pairs={{0,3},{1,2},{2,1},{3,0},{4,7},{5,6},{6,5},{7,4},{8,11},{9,10},{10,... | collective-permute-start | bytes 294920 | tf_op jit(solution)/shard_map/cond/branch_1_fun/ppermute | solution.py:77
  69.2 2.6 %collective-permute-done.39 = bf16[192,256]{1,0:T(8,128)(2,1)S(1)} collective-permute-done((bf16[192,256]{1,0:T(8,128)(2,1)S(1)}, bf16[192,256]{1,0:T(8,128)(2,1)S(1)}, u32[]{:S(2)}, u32[]{:S(2)}) %collective-permute-start.39) | collective-permute-done | bytes 98336 | tf_op jit(solution)/shard_map/cond/branch_1_fun/ppermute | solution.py:77
  72.5 2.4 %collective-permute-start.37 = (f16[256,1024]{1,0:T(8,128)(2,1)S(1)}, f16[256,1024]{1,0:T(8,128)(2,1)S(1)}, u32[]{:S(2)}, u32[]{:S(2)}) collective-permute-start(f16[256,1024]{1,0:T(8,128)(2,1)S(1)} %get-tuple-element.142), channel_id=1, source_target_pairs={{0,8},{4,12},{8,16},{12,20},{16,24},{20,28},{24,0},{28,4},{1,9},{5... | collective-permute-start | bytes 1572872 | tf_op jit(solution)/shard_map/cond/branch_1_fun/ppermute | solution.py:61
  74.8 1.8 %multiply_convert_fusion.13 = (f16[256,1024]{1,0:T(8,128)(2,1)S(1)}, f32[256,1024]{1,0:T(8,128)S(1)}) fusion(bf16[1,1024,1024]{2,1,0:T(8,128)(2,1)S(1)} %copy-done.1, bf16[192,512]{1,0:T(8,128)(2,1)S(1)} %collective-permute-done.31, bf16[192,512]{1,0:T(8,128)(2,1)S(1)} %collective-permute-done.28, bf16[192,512]{1,0:T(8,128)(2,1)S(1)} %collective-permute-done.30, ...), kind=kOutput, calls=%fused_computation.119 | convolution fusion | flops 418906112 | bytes 5111808 | tf_op jit(solution)/shard_map/cond/branch_1_fun/dot_general | solution.py:54
  77.6 1.8 %multiply_convert_fusion.11 = (f16[256,1024]{1,0:T(8,128)(2,1)S(1)}, f32[256,1024]{1,0:T(8,128)S(1)}) fusion(bf16[1,1024,1024]{2,1,0:T(8,128)(2,1)S(1)} %copy-done.1, bf16[192,512]{1,0:T(8,128)(2,1)S(1)} %collective-permute-done.31, bf16[192,512]{1,0:T(8,128)(2,1)S(1)} %collective-permute-done.28, bf16[192,512]{1,0:T(8,128)(2,1)S(1)} %collective-permute-done.30, ...), kind=kOutput, calls=%fused_computation.117 | convolution fusion | flops 418906112 | bytes 5111808 | tf_op jit(solution)/shard_map/cond/branch_1_fun/dot_general | solution.py:54
  82.1 11.1 %collective-permute-done.37 = f16[256,1024]{1,0:T(8,128)(2,1)S(1)} collective-permute-done((f16[256,1024]{1,0:T(8,128)(2,1)S(1)}, f16[256,1024]{1,0:T(8,128)(2,1)S(1)}, u32[]{:S(2)}, u32[]{:S(2)}) %collective-permute-start.37) | collective-permute-done | bytes 524320 | tf_op jit(solution)/shard_map/cond/branch_1_fun/ppermute | solution.py:61
  93.5 8.9 %collective-permute-done.41 = f16[256,1024]{1,0:T(8,128)(2,1)S(1)} collective-permute-done((f16[256,1024]{1,0:T(8,128)(2,1)S(1)}, f16[256,1024]{1,0:T(8,128)(2,1)S(1)}, u32[]{:S(2)}, u32[]{:S(2)}) %collective-permute-start.41) | collective-permute-done | bytes 524320 | tf_op jit(solution)/shard_map/cond/branch_1_fun/ppermute | solution.py:61
  102.7 5.3 %collective-permute-done.45 = f16[256,1024]{1,0:T(8,128)(2,1)S(1)} collective-permute-done((f16[256,1024]{1,0:T(8,128)(2,1)S(1)}, f16[256,1024]{1,0:T(8,128)(2,1)S(1)}, u32[]{:S(2)}, u32[]{:S(2)}) %collective-permute-start.45) | collective-permute-done | bytes 524320 | tf_op jit(solution)/shard_map/cond/branch_1_fun/ppermute | solution.py:61
  (55 shorter events, 19.4 us)
Async XLA Ops:
  2.5 37.3 %copy-start.1 = (bf16[1,1024,1024]{2,1,0:T(8,128)(2,1)S(1)}, bf16[1,1024,1024]{2,1,0:T(8,128)(2,1)}, u32[]{:S(2)}) copy-start(bf16[1,1024,1024]{2,1,0:T(8,128)(2,1)} %get-tuple-element.46) | copy-start | bytes 6291460 | tf_op jit(solution)/shard_map/cond
  2.5 11.1 %collective-permute-start.25 = (bf16[192,256]{1,0:T(8,128)(2,1)S(1)}, bf16[192,256]{1,0:T(8,128)(2,1)S(1)}, u32[]{:S(2)}, u32[]{:S(2)}) collective-permute-start(bf16[192,256]{1,0:T(8,128)(2,1)S(1)} %get-tuple-element.137), channel_id=1, source_target_pairs={{0,3},{1,2},{2,1},{3,0},{4,7},{5,6},{6,5},{7,4},{8,11},{9,10},{10,... | collective-permute-start | bytes 294920 | tf_op jit(solution)/shard_map/cond/branch_1_fun/ppermute | solution.py:77
  7.6 13.4 %collective-permute-start.24 = (bf16[192,256]{1,0:T(8,128)(2,1)S(1)}, bf16[192,256]{1,0:T(8,128)(2,1)S(1)}, u32[]{:S(2)}, u32[]{:S(2)}) collective-permute-start(bf16[192,256]{1,0:T(8,128)(2,1)S(1)} %get-tuple-element.138), channel_id=1, source_target_pairs={{0,2},{1,3},{2,0},{3,1},{4,6},{5,7},{6,4},{7,5},{8,10},{9,11},{10,... | collective-permute-start | bytes 294920 | tf_op jit(solution)/shard_map/cond/branch_1_fun/ppermute | solution.py:77
  7.6 13.4 %collective-permute-start.23 = (bf16[192,256]{1,0:T(8,128)(2,1)S(1)}, bf16[192,256]{1,0:T(8,128)(2,1)S(1)}, u32[]{:S(2)}, u32[]{:S(2)}) collective-permute-start(bf16[192,256]{1,0:T(8,128)(2,1)S(1)} %get-tuple-element.139), channel_id=1, source_target_pairs={{0,1},{1,0},{2,3},{3,2},{4,5},{5,4},{6,7},{7,6},{8,9},{9,8},{10,11... | collective-permute-start | bytes 294920 | tf_op jit(solution)/shard_map/cond/branch_1_fun/ppermute | solution.py:77
  9.2 17.3 %collective-permute-start.27 = (bf16[192,512]{1,0:T(8,128)(2,1)S(1)}, bf16[192,512]{1,0:T(8,128)(2,1)}, u32[]{:S(2)}, u32[]{:S(2)}) collective-permute-start(bf16[192,512]{1,0:T(8,128)(2,1)S(1)} %slice.86), channel_id=1, source_target_pairs={{0,2},{1,3},{2,0},{3,1},{4,6},{5,7},{6,4},{7,5},{8,10},{9,11},{10,... | collective-permute-start | bytes 589832 | tf_op jit(solution)/shard_map/cond/branch_1_fun/ppermute | solution.py:31
  11.6 26.0 %collective-permute-start.26 = (bf16[192,512]{1,0:T(8,128)(2,1)S(1)}, bf16[192,512]{1,0:T(8,128)(2,1)}, u32[]{:S(2)}, u32[]{:S(2)}) collective-permute-start(bf16[192,512]{1,0:T(8,128)(2,1)S(1)} %slice.86), channel_id=1, source_target_pairs={{0,1},{1,0},{2,3},{3,2},{4,5},{5,4},{6,7},{7,6},{8,9},{9,8},{10,11... | collective-permute-start | bytes 589832 | tf_op jit(solution)/shard_map/cond/branch_1_fun/ppermute | solution.py:31
  22.1 54.8 %collective-permute-start.42 = (bf16[192,256]{1,0:T(8,128)(2,1)S(1)}, bf16[192,256]{1,0:T(8,128)(2,1)S(1)}, u32[]{:S(2)}, u32[]{:S(2)}) collective-permute-start(bf16[192,256]{1,0:T(8,128)(2,1)S(1)} %get-tuple-element.126), channel_id=1, source_target_pairs={{0,1},{1,0},{2,3},{3,2},{4,5},{5,4},{6,7},{7,6},{8,9},{9,8},{10,11... | collective-permute-start | bytes 294920 | tf_op jit(solution)/shard_map/cond/branch_1_fun/ppermute | solution.py:77
  22.2 55.3 %collective-permute-start.43 = (bf16[192,256]{1,0:T(8,128)(2,1)S(1)}, bf16[192,256]{1,0:T(8,128)(2,1)S(1)}, u32[]{:S(2)}, u32[]{:S(2)}) collective-permute-start(bf16[192,256]{1,0:T(8,128)(2,1)S(1)} %get-tuple-element.125), channel_id=1, source_target_pairs={{0,2},{1,3},{2,0},{3,1},{4,6},{5,7},{6,4},{7,5},{8,10},{9,11},{10,... | collective-permute-start | bytes 294920 | tf_op jit(solution)/shard_map/cond/branch_1_fun/ppermute | solution.py:77
  26.5 10.0 %collective-permute-start.28 = (bf16[192,512]{1,0:T(8,128)(2,1)}, bf16[192,512]{1,0:T(8,128)(2,1)S(1)}, u32[]{:S(2)}, u32[]{:S(2)}) collective-permute-start(bf16[192,512]{1,0:T(8,128)(2,1)} %collective-permute-done.27), channel_id=1, source_target_pairs={{0,1},{1,0},{2,3},{3,2},{4,5},{5,4},{6,7},{7,6},{8,9},{9,8},{10,11... | collective-permute-start | bytes 589832 | tf_op jit(solution)/shard_map/cond/branch_1_fun/ppermute | solution.py:31
  26.6 13.1 %collective-permute-start.30 = (bf16[192,512]{1,0:T(8,128)(2,1)S(1)}, bf16[192,512]{1,0:T(8,128)(2,1)S(1)}, u32[]{:S(2)}, u32[]{:S(2)}) collective-permute-start(bf16[192,512]{1,0:T(8,128)(2,1)S(1)} %slice.89), channel_id=1, source_target_pairs={{0,2},{1,3},{2,0},{3,1},{4,6},{5,7},{6,4},{7,5},{8,10},{9,11},{10,... | collective-permute-start | bytes 589832 | tf_op jit(solution)/shard_map/cond/branch_1_fun/ppermute | solution.py:31
  36.5 12.9 %collective-permute-start.32 = (bf16[192,512]{1,0:T(8,128)(2,1)S(1)}, bf16[192,512]{1,0:T(8,128)(2,1)S(1)}, u32[]{:S(2)}, u32[]{:S(2)}) collective-permute-start(bf16[192,512]{1,0:T(8,128)(2,1)S(1)} %slice.89), channel_id=1, source_target_pairs={{0,1},{1,0},{2,3},{3,2},{4,5},{5,4},{6,7},{7,6},{8,9},{9,8},{10,11... | collective-permute-start | bytes 589832 | tf_op jit(solution)/shard_map/cond/branch_1_fun/ppermute | solution.py:31
  37.6 21.4 %collective-permute-start.34 = (bf16[192,256]{1,0:T(8,128)(2,1)S(1)}, bf16[192,256]{1,0:T(8,128)(2,1)S(1)}, u32[]{:S(2)}, u32[]{:S(2)}) collective-permute-start(bf16[192,256]{1,0:T(8,128)(2,1)S(1)} %get-tuple-element.134), channel_id=1, source_target_pairs={{0,1},{1,0},{2,3},{3,2},{4,5},{5,4},{6,7},{7,6},{8,9},{9,8},{10,11... | collective-permute-start | bytes 294920 | tf_op jit(solution)/shard_map/cond/branch_1_fun/ppermute | solution.py:77
  39.7 9.1 %collective-permute-start.31 = (bf16[192,512]{1,0:T(8,128)(2,1)S(1)}, bf16[192,512]{1,0:T(8,128)(2,1)S(1)}, u32[]{:S(2)}, u32[]{:S(2)}) collective-permute-start(bf16[192,512]{1,0:T(8,128)(2,1)S(1)} %collective-permute-done.30), channel_id=1, source_target_pairs={{0,1},{1,0},{2,3},{3,2},{4,5},{5,4},{6,7},{7,6},{8,9},{9,8},{10,11... | collective-permute-start | bytes 589832 | tf_op jit(solution)/shard_map/cond/branch_1_fun/ppermute | solution.py:31
  48.7 11.1 %collective-permute-start.35 = (bf16[192,256]{1,0:T(8,128)(2,1)S(1)}, bf16[192,256]{1,0:T(8,128)(2,1)S(1)}, u32[]{:S(2)}, u32[]{:S(2)}) collective-permute-start(bf16[192,256]{1,0:T(8,128)(2,1)S(1)} %get-tuple-element.133), channel_id=1, source_target_pairs={{0,2},{1,3},{2,0},{3,1},{4,6},{5,7},{6,4},{7,5},{8,10},{9,11},{10,... | collective-permute-start | bytes 294920 | tf_op jit(solution)/shard_map/cond/branch_1_fun/ppermute | solution.py:77
  49.4 7.6 %collective-permute-start.29 = (f16[256,512]{1,0:T(8,128)(2,1)S(1)}, f16[256,512]{1,0:T(8,128)(2,1)S(1)}, u32[]{:S(2)}, u32[]{:S(2)}) collective-permute-start(f16[256,512]{1,0:T(8,128)(2,1)S(1)} %get-tuple-element.140), channel_id=1, source_target_pairs={{0,8},{4,12},{8,16},{12,20},{16,24},{20,28},{24,0},{28,4},{1,9},{5... | collective-permute-start | bytes 786440 | tf_op jit(solution)/shard_map/cond/branch_1_fun/ppermute | solution.py:61
  57.0 6.5 %collective-permute-start.36 = (bf16[192,256]{1,0:T(8,128)(2,1)S(1)}, bf16[192,256]{1,0:T(8,128)(2,1)S(1)}, u32[]{:S(2)}, u32[]{:S(2)}) collective-permute-start(bf16[192,256]{1,0:T(8,128)(2,1)S(1)} %get-tuple-element.132), channel_id=1, source_target_pairs={{0,3},{1,2},{2,1},{3,0},{4,7},{5,6},{6,5},{7,4},{8,11},{9,10},{10,... | collective-permute-start | bytes 294920 | tf_op jit(solution)/shard_map/cond/branch_1_fun/ppermute | solution.py:77
  59.0 8.3 %collective-permute-start.38 = (bf16[192,256]{1,0:T(8,128)(2,1)S(1)}, bf16[192,256]{1,0:T(8,128)(2,1)S(1)}, u32[]{:S(2)}, u32[]{:S(2)}) collective-permute-start(bf16[192,256]{1,0:T(8,128)(2,1)S(1)} %get-tuple-element.130), channel_id=1, source_target_pairs={{0,1},{1,0},{2,3},{3,2},{4,5},{5,4},{6,7},{7,6},{8,9},{9,8},{10,11... | collective-permute-start | bytes 294920 | tf_op jit(solution)/shard_map/cond/branch_1_fun/ppermute | solution.py:77
  59.8 12.0 %collective-permute-start.39 = (bf16[192,256]{1,0:T(8,128)(2,1)S(1)}, bf16[192,256]{1,0:T(8,128)(2,1)S(1)}, u32[]{:S(2)}, u32[]{:S(2)}) collective-permute-start(bf16[192,256]{1,0:T(8,128)(2,1)S(1)} %get-tuple-element.129), channel_id=1, source_target_pairs={{0,2},{1,3},{2,0},{3,1},{4,6},{5,7},{6,4},{7,5},{8,10},{9,11},{10,... | collective-permute-start | bytes 294920 | tf_op jit(solution)/shard_map/cond/branch_1_fun/ppermute | solution.py:77
  63.5 8.9 %collective-permute-start.40 = (bf16[192,256]{1,0:T(8,128)(2,1)S(1)}, bf16[192,256]{1,0:T(8,128)(2,1)S(1)}, u32[]{:S(2)}, u32[]{:S(2)}) collective-permute-start(bf16[192,256]{1,0:T(8,128)(2,1)S(1)} %get-tuple-element.128), channel_id=1, source_target_pairs={{0,3},{1,2},{2,1},{3,0},{4,7},{5,6},{6,5},{7,4},{8,11},{9,10},{10,... | collective-permute-start | bytes 294920 | tf_op jit(solution)/shard_map/cond/branch_1_fun/ppermute | solution.py:77
  67.3 10.2 %collective-permute-start.44 = (bf16[192,256]{1,0:T(8,128)(2,1)S(1)}, bf16[192,256]{1,0:T(8,128)(2,1)S(1)}, u32[]{:S(2)}, u32[]{:S(2)}) collective-permute-start(bf16[192,256]{1,0:T(8,128)(2,1)S(1)} %get-tuple-element.124), channel_id=1, source_target_pairs={{0,3},{1,2},{2,1},{3,0},{4,7},{5,6},{6,5},{7,4},{8,11},{9,10},{10,... | collective-permute-start | bytes 294920 | tf_op jit(solution)/shard_map/cond/branch_1_fun/ppermute | solution.py:77
  71.9 10.1 %collective-permute-start.33 = (f16[256,512]{1,0:T(8,128)(2,1)S(1)}, f16[256,512]{1,0:T(8,128)(2,1)S(1)}, u32[]{:S(2)}, u32[]{:S(2)}) collective-permute-start(f16[256,512]{1,0:T(8,128)(2,1)S(1)} %get-tuple-element.122), channel_id=1, source_target_pairs={{0,8},{4,12},{8,16},{12,20},{16,24},{20,28},{24,0},{28,4},{1,9},{5... | collective-permute-start | bytes 786440 | tf_op jit(solution)/shard_map/cond/branch_1_fun/ppermute | solution.py:61
  72.5 20.7 %collective-permute-start.37 = (f16[256,1024]{1,0:T(8,128)(2,1)S(1)}, f16[256,1024]{1,0:T(8,128)(2,1)S(1)}, u32[]{:S(2)}, u32[]{:S(2)}) collective-permute-start(f16[256,1024]{1,0:T(8,128)(2,1)S(1)} %get-tuple-element.142), channel_id=1, source_target_pairs={{0,8},{4,12},{8,16},{12,20},{16,24},{20,28},{24,0},{28,4},{1,9},{5... | collective-permute-start | bytes 1572872 | tf_op jit(solution)/shard_map/cond/branch_1_fun/ppermute | solution.py:61
  76.9 25.5 %collective-permute-start.41 = (f16[256,1024]{1,0:T(8,128)(2,1)S(1)}, f16[256,1024]{1,0:T(8,128)(2,1)S(1)}, u32[]{:S(2)}, u32[]{:S(2)}) collective-permute-start(f16[256,1024]{1,0:T(8,128)(2,1)S(1)} %get-tuple-element.144), channel_id=1, source_target_pairs={{0,8},{4,12},{8,16},{12,20},{16,24},{20,28},{24,0},{28,4},{1,9},{5... | collective-permute-start | bytes 1572872 | tf_op jit(solution)/shard_map/cond/branch_1_fun/ppermute | solution.py:61
  79.3 28.7 %collective-permute-start.45 = (f16[256,1024]{1,0:T(8,128)(2,1)S(1)}, f16[256,1024]{1,0:T(8,128)(2,1)S(1)}, u32[]{:S(2)}, u32[]{:S(2)}) collective-permute-start(f16[256,1024]{1,0:T(8,128)(2,1)S(1)} %get-tuple-element.146), channel_id=1, source_target_pairs={{0,8},{4,12},{8,16},{12,20},{16,24},{20,28},{24,0},{28,4},{1,9},{5... | collective-permute-start | bytes 1572872 | tf_op jit(solution)/shard_map/cond/branch_1_fun/ppermute | solution.py:61
  (4 other events, 57.6 us)
